TPU v7x, 32 devices: a whole 2x2x4 slice. The times are simulated.
32 devices in a mesh: groups: 2 (over x), dp: 16 (over z, y, core).
Axes of the slice: x: 2, y: 2, z: 4, core: 2. Of those that a mesh axis runs over, the one named last changes fastest.
Arguments:
- states: bfloat16 [16384, 1024], P(('groups', 'dp')), parts along dimension 0, may hold values from -6 to 6
- lengths: int32 [64], P(('groups', 'dp')), parts along dimension 0, may hold values from 1 to 256, as said below
- norm_gain: bfloat16 [1024], replicated, may hold values from 0.5 to 2
- w_gate: bfloat16 [1024, 1536], replicated, may hold values from -0.1875 to 0.1875
- w_up: bfloat16 [1024, 1536], replicated, may hold values from -0.1875 to 0.1875
- w_down: bfloat16 [1536, 1024], replicated, may hold values from -0.15625 to 0.15625
- context: bfloat16 [64, 4096], P('groups', 'dp'), parts along dimension 0, may hold values from -6 to 6
- w_out: bfloat16 [4096, 4096], P('dp'), may hold values from -0.09375 to 0.09375
- resid_stream: bfloat16 [64, 4096], P('groups'), parts along dimension 0, may hold values from -6 to 6
- teacher_gain: bfloat16 [4096], replicated, may hold values from 0.5 to 2
Outputs:
- gram_loss: float32 [2], P('groups'), parts along dimension 0
- grad_gate: float32 [2048, 1536], P(('groups', 'dp')), parts along dimension 0
- grad_up: float32 [2048, 1536], P(('groups', 'dp')), parts along dimension 0
- grad_down: float32 [3072, 1024], P(('groups', 'dp')), parts along dimension 0
There are 2 independent parts, one for each index of `groups`. A program takes and returns all parts, laid end to end along the dimension named above; an argument that names none is the same for every part. Nothing has to cross between parts.
Inputs may be any that keep to these rules, and one draw needn't show every extreme that they name: `lengths`: some document of every group fills all 256 slots and some has a single valid token.
All inputs are finite; a program needn't handle non-finite values.
Results may differ from a plain program's by a relative error of at most 0.004.
Values may be sent and summed in bfloat16 or wider, within the bound.
A program may use at most 128 MiB of HBM per device.

v0:
```python
import jax
import jax.numpy as jnp
from jax import lax
from jax.sharding import PartitionSpec as P

EPS = 1e-06
LOSS_SCALE = 4096.0


def teacher_embed(attn_rows, resid_rows, teacher_gain):
    scaled_rows = teacher_gain.astype(jnp.float32) * (resid_rows.astype(jnp.float32) + attn_rows)
    inv_teacher = lax.rsqrt(jnp.sum(scaled_rows * scaled_rows, axis=1, keepdims=True) + EPS)
    return (scaled_rows * inv_teacher).astype(jnp.bfloat16)


def rows_product(left_rows, right_rows):
    return lax.dot_general(
        left_rows, right_rows, (((1,), (1,)), ((), ())), preferred_element_type=jnp.float32
    )


def cols_product(left_cols, right_cols):
    return lax.dot_general(
        left_cols, right_cols, (((0,), (0,)), ((), ())), preferred_element_type=jnp.float32
    )


def per_device(
    states, lengths, norm_gain, w_gate, w_up, w_down, context, w_out, resid_stream, teacher_gain
):
    dp = lax.axis_size("dp")
    my_index = lax.axis_index("dp")
    doc_dev = lengths.shape[0]
    seq_len = states.shape[0] // doc_dev
    model_width = states.shape[1]
    hidden_width = w_gate.shape[1]
    feat = w_out.shape[1] // dp
    high = lax.Precision.HIGHEST
    partial_attn = jnp.dot(context, w_out, preferred_element_type=jnp.float32)
    attn_cols = lax.psum_scatter(partial_attn, "dp", scatter_dimension=1, tiled=True)
    resid_cols = lax.dynamic_slice_in_dim(resid_stream, my_index * feat, feat, 1)
    gain_cols = lax.dynamic_slice_in_dim(teacher_gain, my_index * feat, feat, 0)
    scaled = gain_cols.astype(jnp.float32) * (resid_cols.astype(jnp.float32) + attn_cols)
    gram_part = lax.dot_general(scaled, scaled, (((1,), (1,)), ((), ())), precision=high)
    states_wide = states.astype(jnp.float32)
    inv_rms = lax.rsqrt(jnp.mean(states_wide * states_wide, axis=1, keepdims=True) + EPS)
    normed = (states_wide * inv_rms * norm_gain.astype(jnp.float32)).astype(jnp.bfloat16)
    gate_pre = jnp.dot(normed, w_gate, preferred_element_type=jnp.float32)
    up_pre = jnp.dot(normed, w_up, preferred_element_type=jnp.float32)
    hidden = (jax.nn.silu(gate_pre) * up_pre).astype(jnp.bfloat16)
    positions = lax.broadcasted_iota(jnp.int32, (doc_dev, seq_len), 1)
    valid_mask = (positions < lengths[:, None]).astype(jnp.float32)
    counts = lengths.astype(jnp.float32)
    hidden_sum = jnp.sum(
        hidden.astype(jnp.float32).reshape(doc_dev, seq_len, hidden_width) * valid_mask[:, :, None],
        axis=1,
    )
    state_sum = jnp.sum(
        states_wide.reshape(doc_dev, seq_len, model_width) * valid_mask[:, :, None], axis=1
    )
    packed = jnp.concatenate(
        [hidden_sum, state_sum, jnp.broadcast_to(counts[:, None], (doc_dev, 128))], axis=1
    )
    packed_all = lax.all_gather(packed, "dp", axis=0, tiled=True)
    hidden_all = packed_all[:, :hidden_width]
    state_all = packed_all[:, hidden_width : hidden_width + model_width]
    count_all = packed_all[:, hidden_width + model_width :][:, :1]
    gram_raw = lax.psum(gram_part, "dp")
    docs = gram_raw.shape[0]
    eye = jnp.eye(docs, dtype=jnp.float32)
    inv_col = lax.rsqrt(jnp.sum(gram_raw * eye, axis=1, keepdims=True) + EPS)
    inv_row = lax.rsqrt(jnp.sum(gram_raw * eye, axis=0, keepdims=True) + EPS)
    gram_teacher = gram_raw * inv_col * inv_row
    pooled = (
        state_all + jnp.dot(hidden_all, w_down.astype(jnp.float32), precision=high)
    ) / count_all
    inv_norm = lax.rsqrt(jnp.sum(pooled * pooled, axis=1, keepdims=True) + EPS)
    unit_rows = pooled * inv_norm
    embed = unit_rows.astype(jnp.bfloat16)
    gram_diff = rows_product(embed, embed) - gram_teacher
    diff_norm = jnp.sqrt(jnp.sum(gram_diff * gram_diff) + EPS)
    teacher_norm = jnp.sqrt(jnp.sum(gram_teacher * gram_teacher))
    gram_loss = (diff_norm / teacher_norm).reshape(1)
    d_gram = LOSS_SCALE * gram_diff / (diff_norm * teacher_norm)
    d_embed = 2.0 * jnp.dot(d_gram, embed.astype(jnp.float32), precision=high)
    along = jnp.sum(unit_rows * d_embed, axis=1, keepdims=True)
    d_pooled = (d_embed - unit_rows * along) * inv_norm
    d_all = (d_pooled / count_all).astype(jnp.bfloat16)
    down_rows = hidden_width // dp
    own_hidden = lax.dynamic_slice_in_dim(hidden_all, my_index * down_rows, down_rows, 1)
    grad_down = lax.dot_general(
        own_hidden, d_all.astype(jnp.float32), (((0,), (0,)), ((), ())), precision=high
    )
    d_doc = lax.dynamic_slice_in_dim(d_all, my_index * doc_dev, doc_dev, 0)
    d_hidden = rows_product(d_doc, w_down)
    d_hidden_tok = (d_hidden[:, None, :] * valid_mask[:, :, None]).reshape(
        doc_dev * seq_len, hidden_width
    )
    sigmoid_gate = jax.nn.sigmoid(gate_pre)
    d_gate = (
        d_hidden_tok * up_pre * sigmoid_gate * (1.0 + gate_pre * (1.0 - sigmoid_gate))
    ).astype(jnp.bfloat16)
    d_up = (d_hidden_tok * jax.nn.silu(gate_pre)).astype(jnp.bfloat16)
    rows = model_width // dp
    terms = jnp.concatenate([cols_product(normed, d_gate), cols_product(normed, d_up)], axis=1)
    terms = terms.astype(jnp.bfloat16)
    swapped = lax.all_to_all(terms.reshape(dp, rows, 2 * hidden_width), "dp", 0, 0)
    total = jnp.sum(swapped.astype(jnp.float32), axis=0)
    return (gram_loss, total[:, :hidden_width], total[:, hidden_width:], grad_down)


def solution(mesh):
    in_specs = (
        P(("groups", "dp"), None),
        P(("groups", "dp")),
        P(),
        P(),
        P(),
        P(),
        P("groups", "dp"),
        P("dp", None),
        P("groups", None),
        P(),
    )
    out_specs = (
        P("groups"),
        P(("groups", "dp"), None),
        P(("groups", "dp"), None),
        P(("groups", "dp"), None),
    )
    return jax.shard_map(
        per_device, mesh=mesh, in_specs=in_specs, out_specs=out_specs, check_vma=False
    )
```

profile of v0, /device:TPU:13, one launch (start us, length us, event | category | flops | bytes accessed | tf_op | source)
XLA Modules:
  0.0 300.5 jit_solution(8370609172329494020)
XLA Ops:
  7.2 0.0 copy-start
  7.2 0.0 copy-start.7
  7.2 0.0 copy-start.6
  7.2 0.0 reduce-scatter.2.cloned.1.call-start
  7.2 3.0 %fusion.35 = f32[32,4096]{1,0:T(8,128)} fusion(bf16[32,256]{1,0:T(8,128)(2,1)} %param.16, bf16[256,4096]{1,0:T(8,128)(2,1)} %param.17), kind=kOutput, calls=%fused_computation.65 | convolution fusion | flops 67108864 | bytes 2637824 | tf_op jit(solution)/shard_map/dot_general | solution.py:39
  10.3 0.0 reduce-scatter.2.cloned.1.call-update
  10.3 0.0 copy-done.7
  10.3 0.1 fusion.30
  10.4 1.5 multiply_reduce_fusion.1
  11.9 0.0 copy-done.6
  11.9 1.5 multiply_reduce_fusion
  13.5 0.0 copy-start.3
  13.5 4.2 %fusion.33 = f32[512,1536]{1,0:T(8,128)S(1)} fusion(bf16[1024,1536]{1,0:T(8,128)(2,1)} %param.13, f32[1024]{0:T(1024)S(1)} %convert_element_type.57, f32[512]{0:T(512)S(1)} %add_rsqrt_fusion, bf16[512,1024]{1,0:T(8,128)(2,1)} %param.10), kind=kOutput, calls=%fused_computation.63 | convolution fusion | flops 1612709888 | bytes 7346176 | tf_op jit(solution)/shard_map/dot_general | solution.py:48
  17.7 0.0 copy-done
  17.7 0.0 copy-done.3
  17.7 0.0 copy-start.1
  17.7 3.9 %fusion = (f32[2,1536]{1,0:T(2,128)S(1)}, f32[512,1536]{1,0:T(8,128)}) fusion(f32[2,256]{1,0:T(2,128)S(1)} %get-tuple-element.11, f32[512,1536]{1,0:T(8,128)S(1)} %fusion.33, bf16[1024,1536]{1,0:T(8,128)(2,1)S(1)} %copy-done, f32[1024]{0:T(1024)S(1)} %convert_element_type.57, f32[512]{0:T(512)S(1)} %add_rsqrt_fusion, bf16[512,1024]{1,0:T(8,128)(2,1)S(1)} %copy-done.3), kind=kOutput, calls=%fused_computation.5 | convolution fusion | flops 1619784704 | bytes 10506240 | tf_op jit(solution)/shard_map/dot_general | solution.py:49
  21.6 0.0 copy-done.1
  21.6 0.1 broadcast_in_dim.2
  21.6 18.0 %all-gather = f32[16,2,2688]{2,1,0:T(2,128)} all-gather(f32[1,2,2688]{2,1,0:T(2,128)S(1)} %maximum_bitcast_fusion), channel_id=1, replica_groups=mesh['groups'=2,'dp'=16] {'dp'}, dimensions={0}, use_global_device_ids=true | all-gather | bytes 365568 | tf_op jit(solution)/shard_map/all_gather | solution.py:64
  39.6 1.2 reshape.93
  40.9 0.0 copy-start.5
  40.9 0.8 dynamic-slice_convert_fusion
  41.7 0.0 copy-done.5
  41.7 0.1 slice_reduce_fusion
  41.8 3.7 %multiply_reduce_fusion.3 = (f32[32]{0:T(128)S(1)}, f32[32,1024]{1,0:T(8,128)S(1)}) fusion(f32[32]{0:T(128)S(1)} %slice_reduce_fusion, bf16[1536,1024]{1,0:T(8,128)(2,1)} %param.15, f32[32,2688]{1,0:T(8,128)} %copy-done.5), kind=kOutput, calls=%fused_computation.25 | convolution fusion | flops 604110848 | bytes 3604736 | tf_op jit(solution)/shard_map/dot_general | solution.py:75
  45.5 20.7 %reduce-scatter.2.cloned.1.call-done = f32[32,256]{1,0:T(8,128)} async-done(((f32[32,4096]{1,0:T(8,128)}), f32[32,256]{1,0:T(8,128)}) %reduce-scatter.2.cloned.1.call-update) | async-done | bytes 32784 | tf_op jit(solution)/shard_map/reduce_scatter | solution.py:40
  66.2 1.0 fusion.9
  67.2 45.7 %psum.7 = f32[32,32]{1,0:T(8,128)S(1)} all-reduce(f32[32,32]{1,0:T(8,128)S(1)} %fusion.9), channel_id=1, replica_groups=mesh['groups'=2,'dp'=16] {'dp'}, use_global_device_ids=true, to_apply=%region_5.6 | all-reduce | flops 1024 | bytes 8192 | tf_op jit(solution)/shard_map/psum | solution.py:68
  112.9 0.1 fusion.21
  113.1 0.7 multiply_reduce_fusion.4
  114.4 0.8 multiply_reduce_fusion.5
  116.0 0.0 copy-start.2
  116.0 0.4 multiply_reduce_fusion.2
  116.3 0.1 divide_convert_fusion
  116.4 3.0 %fusion.24 = f32[2,1536]{1,0:T(2,128)S(1)} fusion(bf16[1536,1024]{1,0:T(8,128)(2,1)} %param.15, bf16[32,1024]{1,0:T(8,128)(2,1)S(1)} %divide_convert_fusion, s32[]{:T(128)S(6)} %select_n.11), kind=kOutput, calls=%fused_computation.48 | convolution fusion | flops 6291456 | bytes 3162116 | tf_op jit(solution)/shard_map/dot_general | solution.py:17
  119.5 0.0 copy-done.2
  119.5 3.5 %fusion.5 = (bf16[512,1536]{1,0:T(8,128)(2,1)S(1)}, bf16[512,1536]{1,0:T(8,128)(2,1)S(1)}) fusion(f32[512,1536]{1,0:T(8,128)} %get-tuple-element.13, f32[512,1536]{1,0:T(8,128)S(1)} %copy-done.2, f32[512]{0:T(512)S(1)} %bitcast.38, f32[2,1536]{1,0:T(2,128)S(1)} %fusion.24), kind=kLoop, calls=%fused_computation.11 | loop fusion | flops 11010048 | bytes 9451520 | tf_op jit(solution)/shard_map/convert_element_type | solution.py:102
  123.0 0.0 copy-done.4
  123.0 1.9 convolution_convert_fusion.1
  125.0 1.9 convolution_convert_fusion
  126.9 3.5 %pad_maximum_fusion = bf16[16,64,3072]{2,1,0:T(8,128)(2,1)} fusion(bf16[16,64,1536]{2,1,0:T(8,128)(2,1)S(1)} %bitcast.37, bf16[16,64,1536]{2,1,0:T(8,128)(2,1)S(1)} %bitcast.36), kind=kLoop, calls=%fused_computation.1 | loop fusion | flops 12582912 | bytes 12582912 | tf_op jit(solution)/shard_map/concatenate | solution.py:105
  130.4 19.8 %all-to-all-start = ((bf16[16,64,3072]{2,1,0:T(8,128)(2,1)}), bf16[16,64,3072]{2,1,0:T(8,128)(2,1)}, u32[]{:S(2)}, u32[]{:S(2)}) async-start(bf16[16,64,3072]{2,1,0:T(8,128)(2,1)} %pad_maximum_fusion), calls=%async_computation.1 | async-start | bytes 12582912 | tf_op jit(solution)/shard_map/all_to_all | solution.py:107
  150.2 0.0 slice-done
  150.2 1.2 fusion.13
  151.4 136.2 %all-to-all-done = bf16[16,64,3072]{2,1,0:T(8,128)(2,1)} async-done(((bf16[16,64,3072]{2,1,0:T(8,128)(2,1)}), bf16[16,64,3072]{2,1,0:T(8,128)(2,1)}, u32[]{:S(2)}, u32[]{:S(2)}) %all-to-all-start) | async-done | bytes 6291488 | tf_op jit(solution)/shard_map/all_to_all | solution.py:107
  287.6 4.0 %convert_reduce_fusion = f32[64,3072]{1,0:T(8,128)S(1)} fusion(bf16[16,64,3072]{2,1,0:T(8,128)(2,1)} %all-to-all-done), kind=kLoop, calls=%fused_computation | loop fusion | flops 6094848 | bytes 7077888 | tf_op jit(solution)/shard_map/reduce_sum | solution.py:108
  291.6 0.9 fusion.34
  (9 shorter events, 0.0 us)
Async XLA Ops:
  7.2 10.5 %copy-start = (bf16[1024,1536]{1,0:T(8,128)(2,1)S(1)}, bf16[1024,1536]{1,0:T(8,128)(2,1)}, u32[]{:S(2)}) copy-start(bf16[1024,1536]{1,0:T(8,128)(2,1)} %param.14) | copy-start | bytes 9437188
  7.2 3.1 %copy-start.7 = (s32[2]{0:T(128)S(1)}, s32[2]{0:T(128)}, u32[]{:S(2)}) copy-start(s32[2]{0:T(128)} %param.11) | copy-start | bytes 28
  7.2 4.7 %copy-start.6 = (bf16[1024]{0:T(1024)(128)(2,1)S(1)}, bf16[1024]{0:T(1024)(128)(2,1)}, u32[]{:S(2)}) copy-start(bf16[1024]{0:T(1024)(128)(2,1)} %param.12) | copy-start | bytes 6148
  7.2 59.0 %reduce-scatter.2.cloned.1.call-start = ((), (), s32[]{:S(2)}) async-start(), calls=%async_computation.2 | async-start | bytes 557056 | tf_op jit(solution)/shard_map/reduce_scatter | solution.py:40
  13.5 4.2 %copy-start.3 = (bf16[512,1024]{1,0:T(8,128)(2,1)S(1)}, bf16[512,1024]{1,0:T(8,128)(2,1)}, u32[]{:S(2)}) copy-start(bf16[512,1024]{1,0:T(8,128)(2,1)} %param.10) | copy-start | bytes 3145732
  17.7 3.9 %copy-start.1 = (f32[512,1536]{1,0:T(8,128)}, f32[512,1536]{1,0:T(8,128)S(1)}, u32[]{:S(2)}) copy-start(f32[512,1536]{1,0:T(8,128)S(1)} %fusion.33) | copy-start | bytes 9437188
  40.9 0.8 copy-start.5
  116.0 3.5 %copy-start.2 = (f32[512,1536]{1,0:T(8,128)S(1)}, f32[512,1536]{1,0:T(8,128)}, u32[]{:S(2)}) copy-start(f32[512,1536]{1,0:T(8,128)} %copy-done.1) | copy-start | bytes 9437188
  119.5 3.5 %copy-start.4 = (bf16[512,1024]{1,0:T(8,128)(2,1)S(1)}, bf16[512,1024]{1,0:T(8,128)(2,1)}, u32[]{:S(2)}) copy-start(bf16[512,1024]{1,0:T(8,128)(2,1)} %param.10) | copy-start | bytes 3145732
  130.4 19.8 %slice-start = ((f32[32,2688]{1,0:T(8,128)}), f32[32,1536]{1,0:T(8,128)S(1)}, s32[]{:S(2)}) async-start(f32[32,2688]{1,0:T(8,128)} %copy-done.5), calls=%async_computation.3 | async-start | bytes 393216 | tf_op jit(solution)/shard_map/slice | solution.py:65
  130.4 157.2 %all-to-all-start = ((bf16[16,64,3072]{2,1,0:T(8,128)(2,1)}), bf16[16,64,3072]{2,1,0:T(8,128)(2,1)}, u32[]{:S(2)}, u32[]{:S(2)}) async-start(bf16[16,64,3072]{2,1,0:T(8,128)(2,1)} %pad_maximum_fusion), calls=%async_computation.1 | async-start | bytes 12582912 | tf_op jit(solution)/shard_map/all_to_all | solution.py:107
Sparse Core Ops, SparseCore 0:
  11.6 54.5 reduce-scatter.1
where the time goes:
time: 301 us
  waiting for transfers between devices  157 us (52%)
  blocking collectives  63.7 us (21%)
  matrix products  25.1 us (8%)
  starting transfers between devices  19.8 us (7%)
  between operations  16.8 us (6%)
  other arithmetic  15.9 us (5%)
    all_to_all x1, waiting for transfers between devices, per_device(): lax.all_to_all(terms.reshape(dp, rows, 2 * hidden_width), 'dp', 0, 0)  136 us
    psum x1, blocking collectives, per_device(): gram_raw = lax.psum(gram_part, 'dp')  45.7 us
    reduce_scatter x1, waiting for transfers between devices, per_device(): lax.psum_scatter(partial_attn, 'dp', scatter_dimension=1, tiled=True)  20.7 us
    all_to_all x1, starting transfers between devices, per_device(): lax.all_to_all(terms.reshape(dp, rows, 2 * hidden_width), 'dp', 0, 0)  19.8 us
    all_gather x1, blocking collectives, per_device(): packed_all = lax.all_gather(packed, 'dp', axis=0, tiled=True)  18 us
  transfers between devices with their start and end apart: 2, of which 2 were waited for; matrix products, arithmetic and copies ran while one was open for 6% of the time, Pallas kernels for 0%

commit v1 on v0

--- a/solution.py
+++ b/solution.py
@@ -5,6 +5,11 @@
 
 EPS = 1e-06
 LOSS_SCALE = 4096.0
+
+
+def gather_and_add(array, axis):
+    parts = lax.all_gather(array, axis)
+    return jnp.sum(parts, axis=0)
 
 
 def teacher_embed(attn_rows, resid_rows, teacher_gain):
@@ -65,7 +70,7 @@
     hidden_all = packed_all[:, :hidden_width]
     state_all = packed_all[:, hidden_width : hidden_width + model_width]
     count_all = packed_all[:, hidden_width + model_width :][:, :1]
-    gram_raw = lax.psum(gram_part, "dp")
+    gram_raw = gather_and_add(gram_part, "dp")
     docs = gram_raw.shape[0]
     eye = jnp.eye(docs, dtype=jnp.float32)
     inv_col = lax.rsqrt(jnp.sum(gram_raw * eye, axis=1, keepdims=True) + EPS)

time: 301 us -> 266 us (0.88)
  blocking collectives: 63.7 us -> 36.6 us
  starting transfers between devices: 19.8 us -> 9.43 us
    psum x1 -> x0, blocking collectives: 45.7 us -> none  [per_device(): gram_raw = lax.psum(gram_part, 'dp')]
    all_gather x0 -> x1, blocking collectives: none -> 18.7 us  [gather_and_add(): parts = lax.all_gather(array, axis)]
    all_to_all x1, starting transfers between devices: 19.8 us -> 9.39 us  [per_device(): lax.all_to_all(terms.reshape(dp, rows, 2 * hidden_width), 'dp', 0, 0)]
  transfers between devices with their start and end apart: 2 -> 2, of which waited for: 2 -> 2; matrix products, arithmetic and copies ran while one was open for 6% -> 7% of each run, Pallas kernels for 0% -> 0%
where the time goes in v1:
time: 266 us; the launch traced here: 265 us
  waiting for transfers between devices  155 us (58%)
  blocking collectives  36.6 us (14%)
  matrix products  26.4 us (10%)
  other arithmetic  17.1 us (6%)
  between operations  16.7 us (6%)
  starting transfers between devices  9.43 us (4%)
  local copies, waits for them, and re-layouts  3.58 us (1%)
    all_to_all x1, waiting for transfers between devices, per_device(): lax.all_to_all(terms.reshape(dp, rows, 2 * hidden_width), 'dp', 0, 0)  136 us
    reduce_scatter x1, waiting for transfers between devices, per_device(): lax.psum_scatter(partial_attn, 'dp', scatter_dimension=1, tiled=True)  19 us
    all_gather x1, blocking collectives, gather_and_add(): parts = lax.all_gather(array, axis)  18.7 us
    all_gather x1, blocking collectives, per_device(): packed_all = lax.all_gather(packed, 'dp', axis=0, tiled=True)  18 us
    all_to_all x1, starting transfers between devices, per_device(): lax.all_to_all(terms.reshape(dp, rows, 2 * hidden_width), 'dp', 0, 0)  9.39 us
  transfers between devices with their start and end apart: 2, of which 2 were waited for; matrix products, arithmetic and copies ran while one was open for 7% of the time, Pallas kernels for 0%

profile of v1, /device:TPU:13, one launch (start us, length us, event | category | flops | bytes accessed | tf_op | source)
XLA Modules:
  0.0 265.0 jit_solution(11175572083951547409)
XLA Ops:
  7.2 0.0 copy-start
  7.2 0.0 copy-start.13
  7.2 0.0 copy-start.12
  7.2 0.0 reduce-scatter.2.cloned.1.call-start
  7.2 3.0 %fusion.35 = f32[32,4096]{1,0:T(8,128)} fusion(bf16[32,256]{1,0:T(8,128)(2,1)} %param.16, bf16[256,4096]{1,0:T(8,128)(2,1)} %param.17), kind=kOutput, calls=%fused_computation.65 | convolution fusion | flops 67108864 | bytes 2637824 | tf_op jit(solution)/shard_map/dot_general | solution.py:44
  10.3 0.0 reduce-scatter.2.cloned.1.call-update
  10.3 0.1 fusion.30
  10.4 1.5 multiply_reduce_fusion.1
  11.9 0.0 copy-start.6
  12.0 1.5 multiply_reduce_fusion
  13.5 0.0 copy-start.3
  13.5 4.2 %fusion.33 = f32[512,1536]{1,0:T(8,128)S(1)} fusion(bf16[1024,1536]{1,0:T(8,128)(2,1)} %param.13, f32[1024]{0:T(1024)S(1)} %convert_element_type.57, f32[512]{0:T(512)S(1)} %add_rsqrt_fusion, bf16[512,1024]{1,0:T(8,128)(2,1)} %param.10), kind=kOutput, calls=%fused_computation.63 | convolution fusion | flops 1612709888 | bytes 7346176 | tf_op jit(solution)/shard_map/dot_general | solution.py:53
  17.7 3.9 %fusion = (f32[2,1536]{1,0:T(2,128)S(1)}, f32[512,1536]{1,0:T(8,128)}) fusion(f32[2,256]{1,0:T(2,128)S(1)} %get-tuple-element.11, f32[512,1536]{1,0:T(8,128)S(1)} %fusion.33, bf16[1024,1536]{1,0:T(8,128)(2,1)S(1)} %copy-done, f32[1024]{0:T(1024)S(1)} %convert_element_type.57, f32[512]{0:T(512)S(1)} %add_rsqrt_fusion, bf16[512,1024]{1,0:T(8,128)(2,1)S(1)} %copy-done.3), kind=kOutput, calls=%fused_computation.5 | convolution fusion | flops 1619784704 | bytes 10506240 | tf_op jit(solution)/shard_map/dot_general | solution.py:54
  21.6 0.0 copy-done.1
  21.6 0.1 broadcast_in_dim.2
  21.7 18.0 %all-gather.1 = f32[16,2,2688]{2,1,0:T(2,128)} all-gather(f32[1,2,2688]{2,1,0:T(2,128)S(1)} %maximum_bitcast_fusion), channel_id=1, replica_groups=mesh['groups'=2,'dp'=16] {'dp'}, dimensions={0}, use_global_device_ids=true | all-gather | bytes 365568 | tf_op jit(solution)/shard_map/all_gather | solution.py:69
  39.7 0.6 copy.14
  40.2 1.2 reshape.94
  41.5 0.0 copy-start.5
  41.5 0.8 dynamic-slice_convert_fusion
  42.3 0.1 slice_reduce_fusion
  42.4 0.6 copy-done.11
  43.0 3.7 %multiply_reduce_fusion.3 = (f32[32]{0:T(128)S(1)}, f32[32,1024]{1,0:T(8,128)S(1)}) fusion(f32[32]{0:T(128)S(1)} %slice_reduce_fusion, bf16[1536,1024]{1,0:T(8,128)(2,1)} %param.15, f32[32,2688]{1,0:T(8,128)} %copy-done.5), kind=kOutput, calls=%fused_computation.25 | convolution fusion | flops 604110848 | bytes 3604736 | tf_op jit(solution)/shard_map/dot_general | solution.py:80
  46.7 0.5 add_rsqrt_fusion.3
  47.2 19.0 %reduce-scatter.2.cloned.1.call-done = f32[32,256]{1,0:T(8,128)} async-done(((f32[32,4096]{1,0:T(8,128)}), f32[32,256]{1,0:T(8,128)}) %reduce-scatter.2.cloned.1.call-update) | async-done | bytes 32784 | tf_op jit(solution)/shard_map/reduce_scatter | solution.py:45
  66.2 1.0 fusion.9
  67.2 18.7 %all-gather = f32[512,32]{1,0:T(8,128)S(1)} all-gather(f32[32,32]{1,0:T(8,128)S(1)} %fusion.9), channel_id=2, replica_groups=mesh['groups'=2,'dp'=16] {'dp'}, dimensions={0}, use_global_device_ids=true | all-gather | bytes 69632 | tf_op jit(solution)/shard_map/all_gather | solution.py:11
  85.9 0.0 copy-start.10
  85.9 0.1 fusion.21
  86.1 0.7 multiply_reduce_fusion.4
  87.3 1.6 multiply_reduce_fusion.5
  89.5 1.2 multiply_reduce_fusion.2
  90.7 0.8 divide_convert_fusion
  91.5 2.8 %fusion.24 = f32[2,1536]{1,0:T(2,128)S(1)} fusion(bf16[1536,1024]{1,0:T(8,128)(2,1)} %param.15, bf16[32,1024]{1,0:T(8,128)(2,1)S(1)} %divide_convert_fusion, s32[]{:T(128)S(6)} %select_n.11), kind=kOutput, calls=%fused_computation.48 | convolution fusion | flops 6291456 | bytes 3162116 | tf_op jit(solution)/shard_map/dot_general | solution.py:22
  94.3 0.0 copy-start.4
  94.4 0.0 copy-start.7
  94.4 3.5 %fusion.5 = (bf16[512,1536]{1,0:T(8,128)(2,1)S(1)}, bf16[512,1536]{1,0:T(8,128)(2,1)S(1)}) fusion(f32[512,1536]{1,0:T(8,128)} %get-tuple-element.13, f32[512,1536]{1,0:T(8,128)S(1)} %copy-done.2, f32[512]{0:T(512)S(1)} %bitcast.40, f32[2,1536]{1,0:T(2,128)S(1)} %fusion.24), kind=kLoop, calls=%fused_computation.11 | loop fusion | flops 11010048 | bytes 9451520 | tf_op jit(solution)/shard_map/convert_element_type | solution.py:107
  97.9 0.0 copy-done.4
  97.9 0.0 copy-done.7
  97.9 0.0 copy-done.9
  97.9 1.9 convolution_convert_fusion.1
  99.9 1.9 convolution_convert_fusion
  101.8 3.5 %pad_maximum_fusion = bf16[16,64,3072]{2,1,0:T(8,128)(2,1)} fusion(bf16[16,64,1536]{2,1,0:T(8,128)(2,1)S(1)} %bitcast.38, bf16[16,64,1536]{2,1,0:T(8,128)(2,1)S(1)} %bitcast.37), kind=kLoop, calls=%fused_computation.1 | loop fusion | flops 12582912 | bytes 12582912 | tf_op jit(solution)/shard_map/concatenate | solution.py:110
  105.3 9.4 %all-to-all-start = ((bf16[16,64,3072]{2,1,0:T(8,128)(2,1)}), bf16[16,64,3072]{2,1,0:T(8,128)(2,1)}, u32[]{:S(2)}, u32[]{:S(2)}) async-start(bf16[16,64,3072]{2,1,0:T(8,128)(2,1)} %pad_maximum_fusion), calls=%async_computation.1 | async-start | bytes 12582912 | tf_op jit(solution)/shard_map/all_to_all | solution.py:112
  114.7 1.2 fusion.13
  115.9 136.2 %all-to-all-done = bf16[16,64,3072]{2,1,0:T(8,128)(2,1)} async-done(((bf16[16,64,3072]{2,1,0:T(8,128)(2,1)}), bf16[16,64,3072]{2,1,0:T(8,128)(2,1)}, u32[]{:S(2)}, u32[]{:S(2)}) %all-to-all-start) | async-done | bytes 6291488 | tf_op jit(solution)/shard_map/all_to_all | solution.py:112
  252.1 4.0 %convert_reduce_fusion = f32[64,3072]{1,0:T(8,128)S(1)} fusion(bf16[16,64,3072]{2,1,0:T(8,128)(2,1)} %all-to-all-done), kind=kLoop, calls=%fused_computation | loop fusion | flops 6094848 | bytes 7077888 | tf_op jit(solution)/shard_map/reduce_sum | solution.py:113
  256.1 0.9 fusion.34
  (22 shorter events, 0.1 us)
Async XLA Ops:
  7.2 10.5 %copy-start = (bf16[1024,1536]{1,0:T(8,128)(2,1)S(1)}, bf16[1024,1536]{1,0:T(8,128)(2,1)}, u32[]{:S(2)}) copy-start(bf16[1024,1536]{1,0:T(8,128)(2,1)} %param.14) | copy-start | bytes 9437188
  7.2 3.1 %copy-start.13 = (s32[2]{0:T(128)S(1)}, s32[2]{0:T(128)}, u32[]{:S(2)}) copy-start(s32[2]{0:T(128)} %param.11) | copy-start | bytes 28
  7.2 4.7 %copy-start.12 = (bf16[1024]{0:T(1024)(128)(2,1)S(1)}, bf16[1024]{0:T(1024)(128)(2,1)}, u32[]{:S(2)}) copy-start(bf16[1024]{0:T(1024)(128)(2,1)} %param.12) | copy-start | bytes 6148
  7.2 59.0 %reduce-scatter.2.cloned.1.call-start = ((), (), s32[]{:S(2)}) async-start(), calls=%async_computation.2 | async-start | bytes 557056 | tf_op jit(solution)/shard_map/reduce_scatter | solution.py:45
  11.9 5.8 %copy-start.8 = (f32[512]{0:T(512)}, f32[512]{0:T(512)S(1)}, u32[]{:S(2)}) copy-start(f32[512]{0:T(512)S(1)} %add_rsqrt_fusion) | copy-start | bytes 6148
  11.9 5.7 %copy-start.6 = (f32[1024]{0:T(1024)}, f32[1024]{0:T(1024)S(1)}, u32[]{:S(2)}) copy-start(f32[1024]{0:T(1024)S(1)} %convert_element_type.57) | copy-start | bytes 12292
  13.5 4.2 %copy-start.3 = (bf16[512,1024]{1,0:T(8,128)(2,1)S(1)}, bf16[512,1024]{1,0:T(8,128)(2,1)}, u32[]{:S(2)}) copy-start(bf16[512,1024]{1,0:T(8,128)(2,1)} %param.10) | copy-start | bytes 3145732
  17.7 3.9 %copy-start.1 = (f32[512,1536]{1,0:T(8,128)}, f32[512,1536]{1,0:T(8,128)S(1)}, u32[]{:S(2)}) copy-start(f32[512,1536]{1,0:T(8,128)S(1)} %fusion.33) | copy-start | bytes 9437188
  41.5 0.8 copy-start.5
  42.4 0.6 copy-start.11
  85.9 8.4 %copy-start.10 = (f32[1,2,2,128]{3,1,2,0:T(2,128)S(1)}, f32[1,2,2,128]{3,1,2,0:T(2,128)}, u32[]{:S(2)}) copy-start(f32[1,2,2,128]{3,1,2,0:T(2,128)} %copy.14) | copy-start | bytes 6148
  89.5 4.8 %copy-start.2 = (f32[512,1536]{1,0:T(8,128)S(1)}, f32[512,1536]{1,0:T(8,128)}, u32[]{:S(2)}) copy-start(f32[512,1536]{1,0:T(8,128)} %copy-done.1) | copy-start | bytes 9437188
  94.3 3.6 %copy-start.4 = (bf16[512,1024]{1,0:T(8,128)(2,1)S(1)}, bf16[512,1024]{1,0:T(8,128)(2,1)}, u32[]{:S(2)}) copy-start(bf16[512,1024]{1,0:T(8,128)(2,1)} %param.10) | copy-start | bytes 3145732
  94.4 3.6 %copy-start.7 = (f32[1024]{0:T(1024)S(1)}, f32[1024]{0:T(1024)}, u32[]{:S(2)}) copy-start(f32[1024]{0:T(1024)} %copy-done.6) | copy-start | bytes 12292
  94.4 3.6 %copy-start.9 = (f32[512]{0:T(512)S(1)}, f32[512]{0:T(512)}, u32[]{:S(2)}) copy-start(f32[512]{0:T(512)} %copy-done.8) | copy-start | bytes 6148
  105.3 9.4 %slice-start = ((f32[32,2688]{1,0:T(8,128)}), f32[32,1536]{1,0:T(8,128)S(1)}, s32[]{:S(2)}) async-start(f32[32,2688]{1,0:T(8,128)} %copy-done.5), calls=%async_computation.3 | async-start | bytes 393216 | tf_op jit(solution)/shard_map/slice | solution.py:70
  105.3 146.8 %all-to-all-start = ((bf16[16,64,3072]{2,1,0:T(8,128)(2,1)}), bf16[16,64,3072]{2,1,0:T(8,128)(2,1)}, u32[]{:S(2)}, u32[]{:S(2)}) async-start(bf16[16,64,3072]{2,1,0:T(8,128)(2,1)} %pad_maximum_fusion), calls=%async_computation.1 | async-start | bytes 12582912 | tf_op jit(solution)/shard_map/all_to_all | solution.py:112
Sparse Core Ops, SparseCore 0:
  11.6 54.5 reduce-scatter.1
